TPU v7x, 32 devices: a whole 2x2x4 slice. The times are simulated.
32 devices in a mesh: dp: 16 (over z, x, core), mp: 2 (over y).
Axes of the slice: x: 2, y: 2, z: 4, core: 2. Of those that a mesh axis runs over, the one named last changes fastest.
Arguments:
- tokens: bfloat16 [12544, 768], P(('dp', 'mp')), may hold values from -6 to 6
- tissue: int32 [16, 784], P('dp'), may hold values from 0 to 1, as said below
- first_gain: float32 [768], replicated, may hold values from 0.5 to 1.5
- first_shift: float32 [768], replicated, may hold values from -3 to 3
- w_query: bfloat16 [768, 768], P(None, 'mp'), may hold values from -0.21875 to 0.21875
- b_query: float32 [768], P('mp'), may hold values from -3 to 3
- w_key: bfloat16 [768, 768], P(None, 'mp'), may hold values from -0.21875 to 0.21875
- w_value: bfloat16 [768, 768], P(None, 'mp'), may hold values from -0.21875 to 0.21875
- b_value: float32 [768], P('mp'), may hold values from -3 to 3
- w_output: bfloat16 [768, 768], P('mp'), may hold values from -1.75 to 1.75
- b_output: float32 [768], replicated, may hold values from -3 to 3
- second_gain: float32 [768], replicated, may hold values from 0.5 to 1.5
- second_shift: float32 [768], replicated, may hold values from -3 to 3
- w_upward: bfloat16 [768, 3072], P(None, 'mp'), may hold values from -0.21875 to 0.21875
- b_upward: float32 [3072], P('mp'), may hold values from -3 to 3
- w_down: bfloat16 [3072, 768], P('mp'), may hold values from -0.109375 to 0.109375
- b_down: float32 [768], replicated, may hold values from -3 to 3
- cotangent: bfloat16 [12544, 768], P(('dp', 'mp')), may hold values from -6 to 6
Outputs:
- output: bfloat16 [12544, 768], P(('dp', 'mp'))
- grad_tokens: float32 [12544, 768], P(('dp', 'mp'))
- grad_first_gain: float32 [768], replicated
- grad_first_shift: float32 [768], replicated
- grad_w_query: float32 [768, 768], P(None, 'mp')
- grad_b_query: float32 [768], P('mp')
- grad_w_key: float32 [768, 768], P(None, 'mp')
- grad_w_value: float32 [768, 768], P(None, 'mp')
- grad_b_value: float32 [768], P('mp')
- grad_w_output: float32 [768, 768], P('mp')
- grad_b_output: float32 [768], replicated
- grad_second_gain: float32 [768], replicated
- grad_second_shift: float32 [768], replicated
- grad_w_upward: float32 [768, 3072], P(None, 'mp')
- grad_b_upward: float32 [3072], P('mp')
- grad_w_down: float32 [3072, 768], P('mp')
- grad_b_down: float32 [768], replicated
Inputs may be any that keep to these rules, and one draw needn't show every extreme that they name: `tissue`: every image has from 196 to 784 patches marked 1, in no particular places.
All inputs are finite; a program needn't handle non-finite values.
Results may differ from a plain program's by a relative error of at most 0.015.
Values may be sent and summed in bfloat16 or wider, within the bound.
No kernel may reach another device: no remote copies, remote signals or barrier semaphores. Data moves between devices by JAX's collectives and lax.ppermute only.
A program may use at most 128 MiB of HBM per device.

v0:
```python
import jax
import jax.numpy as jnp
from jax import lax
from jax.sharding import PartitionSpec as P

HEAD = 64
epsilon = 1e-06
masked_score = -1e30


def normalize(values, gain, shift):
    average = jnp.mean(values, axis=-1, keepdims=True)
    centred = values - average
    spread = jnp.mean(centred * centred, axis=-1, keepdims=True)
    return centred * lax.rsqrt(spread + epsilon) * gain + shift


def exact_gelu(values):
    return jax.nn.gelu(values, approximate=False)


def head_layer(
    tokens,
    tissue,
    first_gain,
    first_shift,
    w_query,
    b_query,
    w_key,
    w_value,
    b_value,
    w_output,
    b_output,
    second_gain,
    second_shift,
    w_upward,
    b_upward,
    w_down,
    b_down,
    cotangent,
):
    images = tissue.shape[0]
    patches = tissue.shape[1]
    width_local = w_query.shape[1]
    heads_local = width_local // HEAD
    head_shape = (images, patches, heads_local, HEAD)
    group_rows = images * patches
    scale = HEAD ** (-0.5)
    inputs = tokens.astype(jnp.float32)
    normed1 = normalize(inputs, first_gain, first_shift).astype(jnp.bfloat16)
    gathered1 = lax.all_gather(normed1, "mp", axis=0, tiled=True)
    w_stack = jnp.concatenate([w_query, w_key, w_value], axis=1)
    b_stack = jnp.concatenate([b_query, jnp.zeros_like(b_query), b_value])
    stacked = (jnp.dot(gathered1, w_stack, preferred_element_type=jnp.float32) + b_stack).astype(
        jnp.bfloat16
    )
    queries = stacked[:, :width_local].reshape(head_shape)
    key_rows = stacked[:, width_local : 2 * width_local].reshape(head_shape)
    value_rows = stacked[:, 2 * width_local :].reshape(head_shape)
    valid_keys = (tissue > 0)[:, None, None, :]

    def masked_scores():
        raw_scores = (
            jnp.einsum("ipha,iqha->ihpq", queries, key_rows, preferred_element_type=jnp.float32)
            * scale
        )
        return jnp.where(valid_keys, raw_scores, masked_score)

    scores = masked_scores()
    highest = jnp.max(scores, axis=-1, keepdims=True)
    log_total = highest + jnp.log(jnp.sum(jnp.exp(scores - highest), axis=-1, keepdims=True))
    chance_low = jnp.exp(scores - log_total).astype(jnp.bfloat16)
    context = jnp.einsum(
        "ihpq,iqha->ipha", chance_low, value_rows, preferred_element_type=jnp.float32
    )
    context = context.reshape(group_rows, width_local).astype(jnp.bfloat16)
    part_rows = context
    attention = (
        lax.psum_scatter(
            jnp.dot(part_rows, w_output, preferred_element_type=jnp.float32).astype(jnp.bfloat16),
            "mp",
            scatter_dimension=0,
            tiled=True,
        ).astype(jnp.float32)
        + b_output
    )
    hidden1 = inputs + attention
    normed2 = normalize(hidden1, second_gain, second_shift).astype(jnp.bfloat16)
    gathered2 = lax.all_gather(normed2, "mp", axis=0, tiled=True)
    pre_gelu = jnp.dot(gathered2, w_upward, preferred_element_type=jnp.float32) + b_upward
    activated = exact_gelu(pre_gelu).astype(jnp.bfloat16)
    part_rows = activated
    branch_mlp = (
        lax.psum_scatter(
            jnp.dot(part_rows, w_down, preferred_element_type=jnp.float32).astype(jnp.bfloat16),
            "mp",
            scatter_dimension=0,
            tiled=True,
        ).astype(jnp.float32)
        + b_down
    )
    output = (hidden1 + branch_mlp).astype(jnp.bfloat16)
    grad_rows = lax.all_gather(cotangent, "mp", axis=0, tiled=True)
    grad_down = jnp.einsum("gf,gd->fd", activated, grad_rows, preferred_element_type=jnp.float32)
    grad_active = jnp.einsum("gd,fd->gf", grad_rows, w_down, preferred_element_type=jnp.float32)
    gelu_back = jax.vjp(exact_gelu, pre_gelu)[1]
    grad_pre = gelu_back(grad_active)[0].astype(jnp.bfloat16)
    grad_upward = jnp.einsum("gd,gf->df", gathered2, grad_pre, preferred_element_type=jnp.float32)
    grad_bupward = jnp.sum(grad_pre.astype(jnp.float32), axis=0)
    part_rows = grad_pre
    grad_normed2 = lax.psum_scatter(
        jnp.einsum("gf,df->gd", part_rows, w_upward, preferred_element_type=jnp.float32).astype(
            jnp.bfloat16
        ),
        "mp",
        scatter_dimension=0,
        tiled=True,
    ).astype(jnp.float32)
    norm2_back = jax.vjp(normalize, hidden1, second_gain, second_shift)[1]
    grad_hidden, grad_gain2, grad_shift2 = norm2_back(grad_normed2)
    cotangent_f = cotangent.astype(jnp.float32)
    grad_hidden = grad_hidden + cotangent_f
    grad_bdown = jnp.sum(cotangent_f, axis=0)
    grad_branch = grad_hidden.astype(jnp.bfloat16)
    grad_boutput = jnp.sum(grad_branch.astype(jnp.float32), axis=0)
    grad_columns = lax.all_gather(grad_branch, "mp", axis=0, tiled=True)
    grad_woutput = jnp.einsum(
        "gc,gd->cd", context, grad_columns, preferred_element_type=jnp.float32
    )
    grad_context = jnp.einsum(
        "gd,cd->gc", grad_columns, w_output, preferred_element_type=jnp.float32
    )
    grad_context = grad_context.astype(jnp.bfloat16).reshape(head_shape)
    chances = jnp.exp(masked_scores() - log_total)
    grad_chances = jnp.einsum(
        "ipha,iqha->ihpq", grad_context, value_rows, preferred_element_type=jnp.float32
    )
    grad_value = jnp.einsum(
        "ihpq,ipha->iqha",
        chances.astype(jnp.bfloat16),
        grad_context,
        preferred_element_type=jnp.float32,
    ).astype(jnp.bfloat16)
    grad_scores = chances * (grad_chances - jnp.sum(chances * grad_chances, axis=-1, keepdims=True))
    grad_scores = grad_scores.astype(jnp.bfloat16)
    grad_query = (
        jnp.einsum("ihpq,iqha->ipha", grad_scores, key_rows, preferred_element_type=jnp.float32)
        * scale
    ).astype(jnp.bfloat16)
    grad_key = (
        jnp.einsum("ihpq,ipha->iqha", grad_scores, queries, preferred_element_type=jnp.float32)
        * scale
    ).astype(jnp.bfloat16)
    grad_stack = jnp.concatenate(
        [
            grad_query.reshape(group_rows, width_local),
            grad_key.reshape(group_rows, width_local),
            grad_value.reshape(group_rows, width_local),
        ],
        axis=1,
    )
    grad_wstack = jnp.einsum("gd,gc->dc", gathered1, grad_stack, preferred_element_type=jnp.float32)
    stack_sums = jnp.sum(grad_stack.astype(jnp.float32), axis=0)
    part_rows = grad_stack
    grad_normed1 = lax.psum_scatter(
        jnp.einsum("gc,dc->gd", part_rows, w_stack, preferred_element_type=jnp.float32).astype(
            jnp.bfloat16
        ),
        "mp",
        scatter_dimension=0,
        tiled=True,
    ).astype(jnp.float32)
    norm1_back = jax.vjp(normalize, inputs, first_gain, first_shift)[1]
    grad_inputs, grad_gain1, grad_shift1 = norm1_back(grad_normed1)
    grad_tokens = grad_hidden + grad_inputs
    weight_grads = (
        grad_wstack[:, :width_local],
        stack_sums[:width_local],
        grad_wstack[:, width_local : 2 * width_local],
        grad_wstack[:, 2 * width_local :],
        stack_sums[2 * width_local :],
        grad_woutput,
        grad_upward,
        grad_bupward,
        grad_down,
    )
    small_grads = (grad_gain1, grad_shift1, grad_boutput, grad_gain2, grad_shift2, grad_bdown)
    return (output, grad_tokens, small_grads, weight_grads)


def local(
    tokens,
    tissue,
    first_gain,
    first_shift,
    w_query,
    b_query,
    w_key,
    w_value,
    b_value,
    w_output,
    b_output,
    second_gain,
    second_shift,
    w_upward,
    b_upward,
    w_down,
    b_down,
    cotangent,
):
    arguments = (
        tokens,
        tissue,
        first_gain,
        first_shift,
        w_query,
        b_query,
        w_key,
        w_value,
        b_value,
        w_output,
        b_output,
        second_gain,
        second_shift,
        w_upward,
        b_upward,
        w_down,
        b_down,
        cotangent,
    )
    output, grad_tokens, small_grads, weight_grads = head_layer(*arguments)
    (
        grad_wquery,
        grad_bquery,
        grad_wkey,
        grad_wvalue,
        grad_bvalue,
        grad_woutput,
        grad_upward,
        grad_bupward,
        grad_down,
    ) = weight_grads
    (
        grad_wquery,
        grad_bquery,
        grad_wkey,
        grad_wvalue,
        grad_bvalue,
        grad_woutput,
        grad_upward,
        grad_bupward,
        grad_down,
    ) = lax.psum(
        (
            grad_wquery,
            grad_bquery,
            grad_wkey,
            grad_wvalue,
            grad_bvalue,
            grad_woutput,
            grad_upward,
            grad_bupward,
            grad_down,
        ),
        "dp",
    )
    grad_gain1, grad_shift1, grad_boutput, grad_gain2, grad_shift2, grad_bdown = small_grads
    grad_gain1, grad_shift1, grad_boutput, grad_gain2, grad_shift2, grad_bdown = lax.psum(
        (grad_gain1, grad_shift1, grad_boutput, grad_gain2, grad_shift2, grad_bdown), ("dp", "mp")
    )
    return (
        output,
        grad_tokens,
        grad_gain1,
        grad_shift1,
        grad_wquery,
        grad_bquery,
        grad_wkey,
        grad_wvalue,
        grad_bvalue,
        grad_woutput,
        grad_boutput,
        grad_gain2,
        grad_shift2,
        grad_upward,
        grad_bupward,
        grad_down,
        grad_bdown,
    )


def solution(mesh):
    in_specs = (
        P(("dp", "mp"), None),
        P("dp", None),
        P(),
        P(),
        P(None, "mp"),
        P("mp"),
        P(None, "mp"),
        P(None, "mp"),
        P("mp"),
        P("mp", None),
        P(),
        P(),
        P(),
        P(None, "mp"),
        P("mp"),
        P("mp", None),
        P(),
        P(("dp", "mp"), None),
    )
    out_specs = (
        P(("dp", "mp"), None),
        P(("dp", "mp"), None),
        P(),
        P(),
        P(None, "mp"),
        P("mp"),
        P(None, "mp"),
        P(None, "mp"),
        P("mp"),
        P("mp", None),
        P(),
        P(),
        P(),
        P(None, "mp"),
        P("mp"),
        P("mp", None),
        P(),
    )
    return jax.shard_map(local, mesh=mesh, in_specs=in_specs, out_specs=out_specs, check_vma=False)
```

profile of v0, /device:TPU:0, one launch (start us, length us, event | category | flops | bytes accessed | tf_op | source)
XLA Modules:
  0.0 604.4 jit_solution(9951858389328352436)
XLA Ops:
  17.1 21.1 %all-gather.5.cloned.1.call-done = bf16[784,768]{1,0:T(8,128)(2,1)} async-done(((bf16[392,768]{1,0:T(8,128)(2,1)}), bf16[784,768]{1,0:T(8,128)(2,1)}) %all-gather.5.cloned.1.call-update) | async-done | bytes 1204240 | tf_op jit(solution)/shard_map/all_gather | solution.py:51
  38.2 3.5 fusion.8
  48.5 10.4 %fusion = (f32[6,784]{1,0:T(8,128)S(1)}, f32[6,784,784]{1,2,0:T(8,128)}) fusion(pred[784]{0:T(1024)(128)(4,1)S(1)} %compare_reduce_fusion, bf16[784,6,64]{0,2,1:T(8,128)(2,1)} %bitcast.58, bf16[784,6,64]{0,2,1:T(8,128)(2,1)} %bitcast.60), kind=kOutput, calls=%fused_computation.5 | convolution fusion | flops 483114912 | bytes 15975568 | tf_op jit(solution)/shard_map/ipha,iqha->ihpq/dot_general | solution.py:64
  58.9 9.3 %exponential_reduce_fusion = f32[6,784]{1,0:T(8,128)S(1)} fusion(f32[6,784,784]{1,2,0:T(8,128)} %get-tuple-element.58, f32[6,784]{1,0:T(8,128)S(1)} %get-tuple-element.57, pred[784]{0:T(1024)(128)(4,1)S(1)} %compare_reduce_fusion), kind=kLoop, calls=%fused_computation.3 | loop fusion | flops 14747040 | bytes 14790160 | tf_op jit(solution)/shard_map/reduce_sum | solution.py:71
  68.2 8.2 %fusion.1 = bf16[6,784,784]{1,2,0:T(8,128)(2,1)S(1)} fusion(f32[6,784,784]{1,2,0:T(8,128)} %get-tuple-element.58, f32[6,784]{1,0:T(8,128)S(1)} %log_add_fusion, pred[784]{0:T(1024)(128)(4,1)S(1)} %compare_reduce_fusion), kind=kLoop, calls=%fused_computation.6 | loop fusion | flops 14751744 | bytes 22147216 | tf_op jit(solution)/shard_map/convert_element_type | solution.py:72
  82.5 22.1 %reduce-scatter.5.cloned.1.call-done = bf16[392,768]{1,0:T(8,128)(2,1)} async-done(((bf16[784,768]{1,0:T(8,128)(2,1)}), bf16[392,768]{1,0:T(8,128)(2,1)}) %reduce-scatter.5.cloned.1.call-update) | async-done | bytes 602128 | tf_op jit(solution)/shard_map/reduce_scatter | solution.py:79
  109.4 22.6 %all-gather.7.cloned.1.call-done = bf16[784,768]{1,0:T(8,128)(2,1)} async-done(((bf16[392,768]{1,0:T(8,128)(2,1)}), bf16[784,768]{1,0:T(8,128)(2,1)}) %all-gather.7.cloned.1.call-update) | async-done | bytes 1204240 | tf_op jit(solution)/shard_map/all_gather | solution.py:89
  132.0 6.3 %fusion.39 = f32[784,1536]{1,0:T(8,128)} fusion(bf16[784,768]{1,0:T(8,128)(2,1)} %all-gather.7.cloned.1.call-done, bf16[768,1536]{1,0:T(8,128)(2,1)} %param.31), kind=kOutput, calls=%fused_computation.98 | convolution fusion | flops 1849688064 | bytes 8380416 | tf_op jit(solution)/shard_map/dot_general | solution.py:90
  138.3 18.2 %all-gather.9.cloned.1.call-done = bf16[784,768]{1,0:T(8,128)(2,1)} async-done(((bf16[392,768]{1,0:T(8,128)(2,1)}), bf16[784,768]{1,0:T(8,128)(2,1)}) %all-gather.9.cloned.1.call-update) | async-done | bytes 1204240 | tf_op jit(solution)/shard_map/all_gather | solution.py:103
  156.5 15.6 %convert_reduce_fusion = (f32[1536]{0:T(1024)S(1)}, bf16[784,1536]{1,0:T(8,128)(2,1)S(1)}, f32[784,1536]{1,0:T(8,128)}) fusion(f32[784,1536]{1,0:T(8,128)} %fusion.39, f32[1536]{0:T(1024)S(1)} %copy-done.39, bf16[784,768]{1,0:T(8,128)(2,1)} %all-gather.9.cloned.1.call-done, bf16[1536,768]{1,0:T(8,128)(2,1)S(1)} %copy-done), kind=kOutput, calls=%fused_computation.9 | convolution fusion | flops 1940003328 | bytes 15618048 | tf_op jit(solution)/shard_map/gd,fd->gf/dot_general | solution.py:105
  176.6 5.0 multiply_convert_fusion.1
  183.1 3.1 convolution_convert_fusion.3
  186.3 12.5 %reduce-scatter.9.cloned.1.call-done = bf16[392,768]{1,0:T(8,128)(2,1)} async-done(((bf16[784,768]{1,0:T(8,128)(2,1)}), bf16[392,768]{1,0:T(8,128)(2,1)}) %reduce-scatter.9.cloned.1.call-update) | async-done | bytes 602128 | tf_op jit(solution)/shard_map/reduce_scatter | solution.py:111
  200.6 22.3 %reduce-scatter.7.cloned.1.call-done = bf16[392,768]{1,0:T(8,128)(2,1)} async-done(((bf16[784,768]{1,0:T(8,128)(2,1)}), bf16[392,768]{1,0:T(8,128)(2,1)}) %reduce-scatter.7.cloned.1.call-update) | async-done | bytes 602128 | tf_op jit(solution)/shard_map/reduce_scatter | solution.py:94
  228.1 23.0 %all-gather.11.cloned.1.call-done = bf16[784,768]{1,0:T(8,128)(2,1)} async-done(((bf16[392,768]{1,0:T(8,128)(2,1)}), bf16[784,768]{1,0:T(8,128)(2,1)}) %all-gather.11.cloned.1.call-update) | async-done | bytes 1204240 | tf_op jit(solution)/shard_map/all_gather | solution.py:126
  254.4 6.4 %convolution_convert_fusion.4 = bf16[6,64,784]{2,1,0:T(8,128)(2,1)S(1)} fusion(bf16[784,6,64]{0,2,1:T(8,128)(2,1)} %bitcast.64, bf16[6,784,784]{1,2,0:T(8,128)(2,1)} %copy-done.2), kind=kOutput, calls=%fused_computation.57 | convolution fusion | flops 472356864 | bytes 8580096 | tf_op jit(solution)/shard_map/ihpq,ipha->iqha/dot_general | solution.py:138
  260.9 12.1 %multiply_reduce_fusion = (f32[6,784]{1,0:T(8,128)S(1)}, f32[6,784,784]{1,2,0:T(8,128)}) fusion(f32[6,784,784]{1,2,0:T(8,128)} %get-tuple-element.58, f32[6,784]{1,0:T(8,128)S(1)} %log_add_fusion, pred[784]{0:T(1024)(128)(4,1)S(1)} %compare_reduce_fusion, bf16[784,6,64]{0,2,1:T(8,128)(2,1)S(1)} %bitcast.65, bf16[784,6,64]{0,2,1:T(8,128)(2,1)S(1)} %bitcast.63), kind=kOutput, calls=%fused_computation.1 | convolution fusion | flops 490490784 | bytes 30746128 | tf_op jit(solution)/shard_map/ipha,iqha->ihpq/dot_general | solution.py:135
  273.0 12.3 %multiply_convert_fusion = bf16[6,784,784]{1,2,0:T(8,128)(2,1)S(1)} fusion(f32[6,784,784]{1,2,0:T(8,128)} %get-tuple-element.60, f32[6,784,784]{1,2,0:T(8,128)} %get-tuple-element.58, f32[6,784]{1,0:T(8,128)S(1)} %get-tuple-element.59, f32[6,784]{1,0:T(8,128)S(1)} %log_add_fusion, pred[784]{0:T(1024)(128)(4,1)S(1)} %compare_reduce_fusion), kind=kLoop, calls=%fused_computation | loop fusion | flops 22127616 | bytes 36917776 | tf_op jit(solution)/shard_map/convert_element_type | solution.py:145
  290.6 4.5 convolution_convert_fusion
  295.5 7.0 %fusion.41 = f32[768,1536]{1,0:T(8,128)} fusion(bf16[784,768]{1,0:T(8,128)(2,1)} %all-gather.7.cloned.1.call-done, bf16[784,1536]{1,0:T(8,128)(2,1)} %copy-done.21), kind=kOutput, calls=%fused_computation.100 | convolution fusion | flops 1849688064 | bytes 8331264 | tf_op jit(solution)/shard_map/gd,gf->df/dot_general | solution.py:108
  302.5 4.3 fusion.42
  315.3 64.0 %all-reduce.1 = (f32[384]{0:T(512)}, f32[384]{0:T(512)}, f32[1536]{0:T(1024)}) all-reduce(f32[384]{0:T(512)S(1)} %get-tuple-element.56, f32[384]{0:T(512)S(1)} %get-tuple-element.55, f32[1536]{0:T(1024)S(1)} %get-tuple-element.39), channel_id=1, replica_groups=mesh['dp'=16,'mp'=2] {'dp'}, use_global_device_ids=true, to_apply=%region_21.22 | all-reduce | flops 2304 | bytes 18432 | tf_op jit(solution)/shard_map/psum | solution.py:253
  385.6 39.1 %all-reduce = (f32[768]{0:T(1024)}, f32[768]{0:T(1024)}, f32[768]{0:T(1024)}, f32[768]{0:T(1024)}, f32[768]{0:T(1024)}, /*index=5*/f32[768]{0:T(1024)}) all-reduce(f32[768]{0:T(1024)S(1)} %get-tuple-element.19, f32[768]{0:T(1024)S(1)} %get-tuple-element.22, ...), channel_id=1, replica_groups=mesh['dp'=16,'mp'=2] {'dp','mp'}, use_global_device_ids=true, to_apply=%region_16.17 | all-reduce | flops 4608 | bytes 36864 | tf_op jit(solution)/shard_map/psum | solution.py:268
  424.7 160.7 %all-reduce.5.cloned.1.call-done = (f32[768,384]{1,0:T(8,128)}, f32[768,384]{1,0:T(8,128)}, f32[768,384]{1,0:T(8,128)}, f32[384,768]{1,0:T(8,128)}, f32[768,1536]{1,0:T(8,128)}, /*index=5*/f32[1536,768]{1,0:T(8,128)}) async-done(((f32[768,384]{1,0:T(8,128)}, f32[768,384]{1,0:T(8,128)}, f32[768,384]{1,0:T(8,128)}, f32[384,768]{1,0:T(8,128)}, f32[768,1536]{1,0:T(8,128)}, /*index=5*/f32[1536,768]{1,0:T(8,128)}), ...) | async-done | bytes 14155792 | tf_op jit(solution)/shard_map/psum | solution.py:253
  (169 shorter events, 75.9 us)
Async XLA Ops:
  7.2 149.3 %copy-start = (bf16[1536,768]{1,0:T(8,128)(2,1)S(1)}, bf16[1536,768]{1,0:T(8,128)(2,1)}, u32[]{:S(2)}) copy-start(bf16[1536,768]{1,0:T(8,128)(2,1)} %param.33) | copy-start | bytes 7077892
  7.2 31.0 %all-gather.5.cloned.1.call-start = ((), (), s32[]{:S(2)}) async-start(), calls=%async_computation.4 | async-start | bytes 1806336 | tf_op jit(solution)/shard_map/all_gather | solution.py:51
  12.3 92.3 %reduce-scatter.5.cloned.1.call-start = ((), (), s32[]{:S(2)}) async-start(), calls=%async_computation.5 | async-start | bytes 1806336 | tf_op jit(solution)/shard_map/reduce_scatter | solution.py:79
  79.7 24.9 %copy-start.3 = (bf16[392,768]{1,0:T(8,128)(2,1)S(1)}, bf16[392,768]{1,0:T(8,128)(2,1)}, u32[]{:S(2)}) copy-start(bf16[392,768]{1,0:T(8,128)(2,1)} %param.18) | copy-start | bytes 1806340
  79.7 24.9 %copy-start.30 = (f32[768]{0:T(1024)S(1)}, f32[768]{0:T(1024)}, u32[]{:S(2)}) copy-start(f32[768]{0:T(1024)} %param.28) | copy-start | bytes 9220
  82.4 25.1 %copy-start.34 = (f32[768]{0:T(1024)S(1)}, f32[768]{0:T(1024)}, u32[]{:S(2)}) copy-start(f32[768]{0:T(1024)} %param.29) | copy-start | bytes 9220
  82.4 25.1 %copy-start.40 = (f32[768]{0:T(1024)S(1)}, f32[768]{0:T(1024)}, u32[]{:S(2)}) copy-start(f32[768]{0:T(1024)} %param.30) | copy-start | bytes 9220
  82.5 49.5 %all-gather.7.cloned.1.call-start = ((), (), s32[]{:S(2)}) async-start(), calls=%async_computation.6 | async-start | bytes 1806336 | tf_op jit(solution)/shard_map/all_gather | solution.py:89
  108.7 47.7 %all-gather.9.cloned.1.call-start = ((), (), s32[]{:S(2)}) async-start(), calls=%async_computation.8 | async-start | bytes 1806336 | tf_op jit(solution)/shard_map/all_gather | solution.py:103
  109.3 47.1 %copy-start.39 = (f32[1536]{0:T(1024)S(1)}, f32[1536]{0:T(1024)}, u32[]{:S(2)}) copy-start(f32[1536]{0:T(1024)} %param.32) | copy-start | bytes 18436
  109.3 89.4 %reduce-scatter.9.cloned.1.call-start = ((), (), s32[]{:S(2)}) async-start(), calls=%async_computation.9 | async-start | bytes 1806336 | tf_op jit(solution)/shard_map/reduce_scatter | solution.py:111
  156.5 17.0 %copy-start.43 = (bf16[768,1536]{1,0:T(8,128)(2,1)S(1)}, bf16[768,1536]{1,0:T(8,128)(2,1)}, u32[]{:S(2)}) copy-start(bf16[768,1536]{1,0:T(8,128)(2,1)} %param.31) | copy-start | bytes 7077892
  176.6 46.3 %reduce-scatter.7.cloned.1.call-start = ((), (), s32[]{:S(2)}) async-start(), calls=%async_computation.7 | async-start | bytes 1806336 | tf_op jit(solution)/shard_map/reduce_scatter | solution.py:94
  186.2 36.7 %copy-start.5 = (bf16[392,768]{1,0:T(8,128)(2,1)S(1)}, bf16[392,768]{1,0:T(8,128)(2,1)}, u32[]{:S(2)}) copy-start(bf16[392,768]{1,0:T(8,128)(2,1)} %reduce-scatter.5.cloned.1.call-done) | copy-start | bytes 1806340
  186.2 36.7 %copy-start.41 = (f32[768]{0:T(1024)S(1)}, f32[768]{0:T(1024)}, u32[]{:S(2)}) copy-start(f32[768]{0:T(1024)} %param.34) | copy-start | bytes 9220
  186.2 64.8 %all-gather.11.cloned.1.call-start = ((), (), s32[]{:S(2)}) async-start(), calls=%async_computation.10 | async-start | bytes 1806336 | tf_op jit(solution)/shard_map/all_gather | solution.py:126
  227.8 151.5 %reduce-scatter.11.cloned.1.call-start = ((), (), s32[]{:S(2)}) async-start(), calls=%async_computation.11 | async-start | bytes 1806336 | tf_op jit(solution)/shard_map/reduce_scatter | solution.py:165
  260.9 28.9 %copy-start.13 = (bf16[6,64,784]{2,1,0:T(8,128)(2,1)}, bf16[6,64,784]{2,1,0:T(8,128)(2,1)S(1)}, u32[]{:S(2)}) copy-start(bf16[6,64,784]{2,1,0:T(8,128)(2,1)S(1)} %convolution_convert_fusion.4) | copy-start | bytes 1806340
  273.0 12.3 %copy-start.6 = (bf16[784,384]{0,1:T(8,128)(2,1)S(1)}, bf16[784,384]{0,1:T(8,128)(2,1)}, u32[]{:S(2)}) copy-start(bf16[784,384]{0,1:T(8,128)(2,1)} %copy.48) | copy-start | bytes 1806340
  295.1 290.3 %all-reduce.5.cloned.1.call-start = ((), (), s32[]{:S(2)}) async-start(), calls=%async_computation.12 | async-start | bytes 28311552 | tf_op jit(solution)/shard_map/psum | solution.py:253
  313.3 66.1 %copy-start.32 = (f32[392]{0:T(512)S(1)}, f32[392]{0:T(512)}, u32[]{:S(2)}) copy-start(f32[392]{0:T(512)} %copy-done.31) | copy-start | bytes 4708
  313.3 66.1 %copy-start.33 = (f32[768]{0:T(1024)S(1)}, f32[768]{0:T(1024)}, u32[]{:S(2)}) copy-start(f32[768]{0:T(1024)} %param.20) | copy-start | bytes 9220
  313.4 67.7 %copy-start.38 = (f32[392]{0:T(512)S(1)}, f32[392]{0:T(512)}, u32[]{:S(2)}) copy-start(f32[392]{0:T(512)} %copy-done.37) | copy-start | bytes 4708
  313.4 67.7 %copy-start.36 = (f32[392]{0:T(512)S(1)}, f32[392]{0:T(512)}, u32[]{:S(2)}) copy-start(f32[392]{0:T(512)} %copy-done.35) | copy-start | bytes 4708
  (35 other events, 144.5 us)
Sparse Core Ops, SparseCore 0:
  12.4 25.7 all-gather.4
  82.6 22.0 reduce-scatter.4
  108.9 23.0 all-gather.6
  133.4 23.0 all-gather.8
  176.7 22.0 reduce-scatter.8
  200.8 22.0 reduce-scatter.6
  228.0 23.0 all-gather.10
  295.3 22.0 reduce-scatter.10
  323.6 261.7 all-reduce.4
where the time goes:
time: 613 us; the launch traced here: 604 us
  waiting for transfers between devices  303 us (49%)
  blocking collectives  103 us (17%)
  matrix products  90.6 us (15%)
  other arithmetic  60.8 us (10%)
  local copies, waits for them, and re-layouts  31.1 us (5%)
  between operations  14.8 us (2%)
    psum x1, waiting for transfers between devices, local(): lax.psum((grad_wquery, grad_bquery, grad_wkey, grad_wvalue, grad_bvalue,...  161 us
    psum x1, blocking collectives, local(): lax.psum((grad_wquery, grad_bquery, grad_wkey, grad_wvalue, grad_bvalue,...  64 us
    psum x1, blocking collectives, local(): lax.psum((grad_gain1, grad_shift1, grad_boutput, grad_gain2, grad_shift2,...  39.1 us
    all_gather x1, waiting for transfers between devices, head_layer(): grad_columns = lax.all_gather(grad_branch, 'mp', axis=0, tiled=True)  23 us
    all_gather x1, waiting for transfers between devices, head_layer(): gathered2 = lax.all_gather(normed2, 'mp', axis=0, tiled=True)  22.6 us
    reduce_scatter x1, waiting for transfers between devices, head_layer(): lax.psum_scatter(jnp.dot(part_rows, w_down, preferred_element_type=jnp.fl...  22.3 us
    reduce_scatter x1, waiting for transfers between devices, head_layer(): lax.psum_scatter(jnp.dot(part_rows, w_output, preferred_element_type=jnp....  22.1 us
    all_gather x1, waiting for transfers between devices, head_layer(): gathered1 = lax.all_gather(normed1, 'mp', axis=0, tiled=True)  21.1 us
  transfers between devices with their start and end apart: 9, of which 8 were waited for; matrix products, arithmetic and copies ran while one was open for 8% of the time, Pallas kernels for 0%

commit v1 on v0

--- a/solution.py
+++ b/solution.py
@@ -6,6 +6,30 @@
 HEAD = 64
 epsilon = 1e-06
 masked_score = -1e30
+
+
+def choose_positions(point, dimension_no):
+    point = jnp.moveaxis(point, 0, dimension_no)
+    val = point.shape
+    next_value = point.reshape(
+        *val[:dimension_no], val[dimension_no] * val[dimension_no + 1], *val[dimension_no + 2 :]
+    )
+    return next_value
+
+
+def targets_define(xx, link_axis):
+    h_now, w2 = (lax.axis_size(link_axis), lax.axis_index(link_axis))
+    heard, part_next = (xx[None], 1)
+    while part_next < h_now:
+        seen_now = lax.ppermute(
+            heard, axis_name=link_axis, perm=tuple(((num, num ^ part_next) for num in range(h_now)))
+        )
+        shaped = w2 & part_next == 0
+        heard = jnp.concatenate(
+            [jnp.where(shaped, heard, seen_now), jnp.where(shaped, seen_now, heard)]
+        )
+        part_next *= 2
+    return heard
 
 
 def normalize(values, gain, shift):
@@ -123,7 +147,7 @@
     grad_bdown = jnp.sum(cotangent_f, axis=0)
     grad_branch = grad_hidden.astype(jnp.bfloat16)
     grad_boutput = jnp.sum(grad_branch.astype(jnp.float32), axis=0)
-    grad_columns = lax.all_gather(grad_branch, "mp", axis=0, tiled=True)
+    grad_columns = choose_positions(targets_define(grad_branch, "mp"), 0)
     grad_woutput = jnp.einsum(
         "gc,gd->cd", context, grad_columns, preferred_element_type=jnp.float32
     )

time: 613 us -> 606 us (0.989)
  waiting for transfers between devices: 303 us -> 296 us
    all_gather x1 -> x0, waiting for transfers between devices: 23 us -> none  [head_layer(): grad_columns = lax.all_gather(grad_branch, 'mp', axis=0, tiled=True)]
    ppermute x0 -> x1, waiting for transfers between devices: none -> 15.1 us  [targets_define(): lax.ppermute(heard, axis_name=link_axis, perm=tuple(((num, num ^ part_nex...]
    unnamed x108 -> x112, local copies, waits for them, and re-layouts: 20.5 us -> 21.6 us
where the time goes in v1:
time: 606 us; the launch traced here: 597 us
  waiting for transfers between devices  296 us (49%)
  blocking collectives  102 us (17%)
  matrix products  89.5 us (15%)
  other arithmetic  61.3 us (10%)
  local copies, waits for them, and re-layouts  32.2 us (5%)
  between operations  14.8 us (2%)
    psum x1, waiting for transfers between devices, local(): lax.psum((grad_wquery, grad_bquery, grad_wkey, grad_wvalue, grad_bvalue,...  162 us
    psum x1, blocking collectives, local(): lax.psum((grad_wquery, grad_bquery, grad_wkey, grad_wvalue, grad_bvalue,...  63 us
    psum x1, blocking collectives, local(): lax.psum((grad_gain1, grad_shift1, grad_boutput, grad_gain2, grad_shift2,...  39.1 us
    all_gather x1, waiting for transfers between devices, head_layer(): gathered2 = lax.all_gather(normed2, 'mp', axis=0, tiled=True)  22.6 us
    reduce_scatter x1, waiting for transfers between devices, head_layer(): lax.psum_scatter(jnp.dot(part_rows, w_down, preferred_element_type=jnp.fl...  22.3 us
    reduce_scatter x1, waiting for transfers between devices, head_layer(): lax.psum_scatter(jnp.dot(part_rows, w_output, preferred_element_type=jnp....  22.1 us
    unnamed x112, local copies, waits for them, and re-layouts  21.6 us
    all_gather x1, waiting for transfers between devices, head_layer(): gathered1 = lax.all_gather(normed1, 'mp', axis=0, tiled=True)  21.1 us
  transfers between devices with their start and end apart: 9, of which 8 were waited for; matrix products, arithmetic and copies ran while one was open for 8% of the time, Pallas kernels for 0%

profile of v1, /device:TPU:0, one launch (start us, length us, event | category | flops | bytes accessed | tf_op | source)
XLA Modules:
  0.0 597.0 jit_solution(5678503648696808166)
XLA Ops:
  17.1 21.1 %all-gather.4.cloned.1.call-done = bf16[784,768]{1,0:T(8,128)(2,1)} async-done(((bf16[392,768]{1,0:T(8,128)(2,1)}), bf16[784,768]{1,0:T(8,128)(2,1)}) %all-gather.4.cloned.1.call-update) | async-done | bytes 1204240 | tf_op jit(solution)/shard_map/all_gather | solution.py:75
  38.2 3.5 fusion.8
  48.5 10.4 %fusion = (f32[6,784]{1,0:T(8,128)S(1)}, f32[6,784,784]{1,2,0:T(8,128)}) fusion(pred[784]{0:T(1024)(128)(4,1)S(1)} %compare_reduce_fusion, bf16[784,6,64]{0,2,1:T(8,128)(2,1)} %bitcast.62, bf16[784,6,64]{0,2,1:T(8,128)(2,1)} %bitcast.64), kind=kOutput, calls=%fused_computation.5 | convolution fusion | flops 483114912 | bytes 15975568 | tf_op jit(solution)/shard_map/ipha,iqha->ihpq/dot_general | solution.py:88
  58.9 9.3 %exponential_reduce_fusion = f32[6,784]{1,0:T(8,128)S(1)} fusion(f32[6,784,784]{1,2,0:T(8,128)} %get-tuple-element.60, f32[6,784]{1,0:T(8,128)S(1)} %get-tuple-element.59, pred[784]{0:T(1024)(128)(4,1)S(1)} %compare_reduce_fusion), kind=kLoop, calls=%fused_computation.3 | loop fusion | flops 14747040 | bytes 14790160 | tf_op jit(solution)/shard_map/reduce_sum | solution.py:95
  68.2 8.2 %fusion.1 = bf16[6,784,784]{1,2,0:T(8,128)(2,1)S(1)} fusion(f32[6,784,784]{1,2,0:T(8,128)} %get-tuple-element.60, f32[6,784]{1,0:T(8,128)S(1)} %log_add_fusion, pred[784]{0:T(1024)(128)(4,1)S(1)} %compare_reduce_fusion), kind=kLoop, calls=%fused_computation.6 | loop fusion | flops 14751744 | bytes 22147216 | tf_op jit(solution)/shard_map/convert_element_type | solution.py:96
  82.5 22.1 %reduce-scatter.5.cloned.1.call-done = bf16[392,768]{1,0:T(8,128)(2,1)} async-done(((bf16[784,768]{1,0:T(8,128)(2,1)}), bf16[392,768]{1,0:T(8,128)(2,1)}) %reduce-scatter.5.cloned.1.call-update) | async-done | bytes 602128 | tf_op jit(solution)/shard_map/reduce_scatter | solution.py:103
  109.4 22.6 %all-gather.6.cloned.1.call-done = bf16[784,768]{1,0:T(8,128)(2,1)} async-done(((bf16[392,768]{1,0:T(8,128)(2,1)}), bf16[784,768]{1,0:T(8,128)(2,1)}) %all-gather.6.cloned.1.call-update) | async-done | bytes 1204240 | tf_op jit(solution)/shard_map/all_gather | solution.py:113
  132.0 6.3 %fusion.39 = f32[784,1536]{1,0:T(8,128)} fusion(bf16[784,768]{1,0:T(8,128)(2,1)} %all-gather.6.cloned.1.call-done, bf16[768,1536]{1,0:T(8,128)(2,1)} %param.31), kind=kOutput, calls=%fused_computation.101 | convolution fusion | flops 1849688064 | bytes 8380416 | tf_op jit(solution)/shard_map/dot_general | solution.py:114
  138.3 18.2 %all-gather.8.cloned.1.call-done = bf16[784,768]{1,0:T(8,128)(2,1)} async-done(((bf16[392,768]{1,0:T(8,128)(2,1)}), bf16[784,768]{1,0:T(8,128)(2,1)}) %all-gather.8.cloned.1.call-update) | async-done | bytes 1204240 | tf_op jit(solution)/shard_map/all_gather | solution.py:127
  156.5 15.6 %convert_reduce_fusion = (f32[1536]{0:T(1024)S(1)}, bf16[784,1536]{1,0:T(8,128)(2,1)S(1)}, f32[784,1536]{1,0:T(8,128)}) fusion(f32[784,1536]{1,0:T(8,128)} %fusion.39, f32[1536]{0:T(1024)S(1)} %copy-done.41, bf16[784,768]{1,0:T(8,128)(2,1)} %all-gather.8.cloned.1.call-done, bf16[1536,768]{1,0:T(8,128)(2,1)S(1)} %copy-done), kind=kOutput, calls=%fused_computation.9 | convolution fusion | flops 1940003328 | bytes 15618048 | tf_op jit(solution)/shard_map/gd,fd->gf/dot_general | solution.py:129
  176.8 5.0 multiply_convert_fusion.1
  183.3 3.1 convolution_convert_fusion.3
  186.5 12.2 %reduce-scatter.9.cloned.1.call-done = bf16[392,768]{1,0:T(8,128)(2,1)} async-done(((bf16[784,768]{1,0:T(8,128)(2,1)}), bf16[392,768]{1,0:T(8,128)(2,1)}) %reduce-scatter.9.cloned.1.call-update) | async-done | bytes 602128 | tf_op jit(solution)/shard_map/reduce_scatter | solution.py:135
  200.7 22.3 %reduce-scatter.7.cloned.1.call-done = bf16[392,768]{1,0:T(8,128)(2,1)} async-done(((bf16[784,768]{1,0:T(8,128)(2,1)}), bf16[392,768]{1,0:T(8,128)(2,1)}) %reduce-scatter.7.cloned.1.call-update) | async-done | bytes 602128 | tf_op jit(solution)/shard_map/reduce_scatter | solution.py:118
  227.4 15.1 %collective-permute-done = bf16[1,392,768]{2,1,0:T(8,128)(2,1)} collective-permute-done((bf16[1,392,768]{2,1,0:T(8,128)(2,1)S(1)}, bf16[1,392,768]{2,1,0:T(8,128)(2,1)}, u32[]{:S(2)}, u32[]{:S(2)}) %collective-permute-start) | collective-permute-done | bytes 602144 | tf_op jit(solution)/shard_map/ppermute | solution.py:24
  246.8 6.4 %convolution_convert_fusion.4 = bf16[6,64,784]{2,1,0:T(8,128)(2,1)S(1)} fusion(bf16[784,6,64]{0,2,1:T(8,128)(2,1)} %bitcast.68, bf16[6,784,784]{1,2,0:T(8,128)(2,1)} %copy-done.2), kind=kOutput, calls=%fused_computation.57 | convolution fusion | flops 472356864 | bytes 8580096 | tf_op jit(solution)/shard_map/ihpq,ipha->iqha/dot_general | solution.py:162
  253.3 12.2 %multiply_reduce_fusion = (f32[6,784]{1,0:T(8,128)S(1)}, f32[6,784,784]{1,2,0:T(8,128)}) fusion(f32[6,784,784]{1,2,0:T(8,128)} %get-tuple-element.60, f32[6,784]{1,0:T(8,128)S(1)} %log_add_fusion, pred[784]{0:T(1024)(128)(4,1)S(1)} %compare_reduce_fusion, bf16[784,6,64]{0,2,1:T(8,128)(2,1)S(1)} %bitcast.69, bf16[784,6,64]{0,2,1:T(8,128)(2,1)S(1)} %bitcast.67), kind=kOutput, calls=%fused_computation.1 | convolution fusion | flops 490490784 | bytes 30746128 | tf_op jit(solution)/shard_map/ipha,iqha->ihpq/dot_general | solution.py:159
  265.5 12.3 %multiply_convert_fusion = bf16[6,784,784]{1,2,0:T(8,128)(2,1)S(1)} fusion(f32[6,784,784]{1,2,0:T(8,128)} %get-tuple-element.62, f32[6,784,784]{1,2,0:T(8,128)} %get-tuple-element.60, f32[6,784]{1,0:T(8,128)S(1)} %get-tuple-element.61, f32[6,784]{1,0:T(8,128)S(1)} %log_add_fusion, pred[784]{0:T(1024)(128)(4,1)S(1)} %compare_reduce_fusion), kind=kLoop, calls=%fused_computation | loop fusion | flops 22127616 | bytes 36917776 | tf_op jit(solution)/shard_map/convert_element_type | solution.py:169
  283.2 4.5 convolution_convert_fusion
  287.7 7.0 %fusion.41 = f32[768,1536]{1,0:T(8,128)} fusion(bf16[784,768]{1,0:T(8,128)(2,1)} %all-gather.6.cloned.1.call-done, bf16[784,1536]{1,0:T(8,128)(2,1)} %copy-done.21), kind=kOutput, calls=%fused_computation.103 | convolution fusion | flops 1849688064 | bytes 8331264 | tf_op jit(solution)/shard_map/gd,gf->df/dot_general | solution.py:132
  294.8 4.5 fusion.42
  307.7 63.0 %all-reduce.1 = (f32[384]{0:T(512)}, f32[384]{0:T(512)}, f32[1536]{0:T(1024)}) all-reduce(f32[384]{0:T(512)S(1)} %get-tuple-element.58, f32[384]{0:T(512)S(1)} %get-tuple-element.57, f32[1536]{0:T(1024)S(1)} %get-tuple-element.39), channel_id=1, replica_groups=mesh['dp'=16,'mp'=2] {'dp'}, use_global_device_ids=true, to_apply=%region_21.22 | all-reduce | flops 2304 | bytes 18432 | tf_op jit(solution)/shard_map/psum | solution.py:277
  376.9 39.1 %all-reduce = (f32[768]{0:T(1024)}, f32[768]{0:T(1024)}, f32[768]{0:T(1024)}, f32[768]{0:T(1024)}, f32[768]{0:T(1024)}, /*index=5*/f32[768]{0:T(1024)}) all-reduce(f32[768]{0:T(1024)S(1)} %get-tuple-element.19, f32[768]{0:T(1024)S(1)} %get-tuple-element.22, ...), channel_id=1, replica_groups=mesh['dp'=16,'mp'=2] {'dp','mp'}, use_global_device_ids=true, to_apply=%region_16.17 | all-reduce | flops 4608 | bytes 36864 | tf_op jit(solution)/shard_map/psum | solution.py:292
  416.1 161.8 %all-reduce.5.cloned.1.call-done = (f32[768,384]{1,0:T(8,128)}, f32[768,384]{1,0:T(8,128)}, f32[768,384]{1,0:T(8,128)}, f32[384,768]{1,0:T(8,128)}, f32[768,1536]{1,0:T(8,128)}, /*index=5*/f32[1536,768]{1,0:T(8,128)}) async-done(((f32[768,384]{1,0:T(8,128)}, f32[768,384]{1,0:T(8,128)}, f32[768,384]{1,0:T(8,128)}, f32[384,768]{1,0:T(8,128)}, f32[768,1536]{1,0:T(8,128)}, /*index=5*/f32[1536,768]{1,0:T(8,128)}), ...) | async-done | bytes 14155792 | tf_op jit(solution)/shard_map/psum | solution.py:277
  (174 shorter events, 76.1 us)
Async XLA Ops:
  7.2 149.3 %copy-start = (bf16[1536,768]{1,0:T(8,128)(2,1)S(1)}, bf16[1536,768]{1,0:T(8,128)(2,1)}, u32[]{:S(2)}) copy-start(bf16[1536,768]{1,0:T(8,128)(2,1)} %param.33) | copy-start | bytes 7077892
  7.2 31.0 %all-gather.4.cloned.1.call-start = ((), (), s32[]{:S(2)}) async-start(), calls=%async_computation.4 | async-start | bytes 1806336 | tf_op jit(solution)/shard_map/all_gather | solution.py:75
  12.3 92.3 %reduce-scatter.5.cloned.1.call-start = ((), (), s32[]{:S(2)}) async-start(), calls=%async_computation.5 | async-start | bytes 1806336 | tf_op jit(solution)/shard_map/reduce_scatter | solution.py:103
  79.7 24.9 %copy-start.3 = (bf16[392,768]{1,0:T(8,128)(2,1)S(1)}, bf16[392,768]{1,0:T(8,128)(2,1)}, u32[]{:S(2)}) copy-start(bf16[392,768]{1,0:T(8,128)(2,1)} %param.18) | copy-start | bytes 1806340
  79.8 24.9 %copy-start.32 = (f32[768]{0:T(1024)S(1)}, f32[768]{0:T(1024)}, u32[]{:S(2)}) copy-start(f32[768]{0:T(1024)} %param.28) | copy-start | bytes 9220
  82.5 25.1 %copy-start.36 = (f32[768]{0:T(1024)S(1)}, f32[768]{0:T(1024)}, u32[]{:S(2)}) copy-start(f32[768]{0:T(1024)} %param.29) | copy-start | bytes 9220
  82.5 25.1 %copy-start.42 = (f32[768]{0:T(1024)S(1)}, f32[768]{0:T(1024)}, u32[]{:S(2)}) copy-start(f32[768]{0:T(1024)} %param.30) | copy-start | bytes 9220
  82.5 49.5 %all-gather.6.cloned.1.call-start = ((), (), s32[]{:S(2)}) async-start(), calls=%async_computation.6 | async-start | bytes 1806336 | tf_op jit(solution)/shard_map/all_gather | solution.py:113
  108.8 47.7 %all-gather.8.cloned.1.call-start = ((), (), s32[]{:S(2)}) async-start(), calls=%async_computation.8 | async-start | bytes 1806336 | tf_op jit(solution)/shard_map/all_gather | solution.py:127
  109.3 47.1 %copy-start.41 = (f32[1536]{0:T(1024)S(1)}, f32[1536]{0:T(1024)}, u32[]{:S(2)}) copy-start(f32[1536]{0:T(1024)} %param.32) | copy-start | bytes 18436
  109.3 89.4 %reduce-scatter.9.cloned.1.call-start = ((), (), s32[]{:S(2)}) async-start(), calls=%async_computation.9 | async-start | bytes 1806336 | tf_op jit(solution)/shard_map/reduce_scatter | solution.py:135
  156.5 17.0 %copy-start.45 = (bf16[768,1536]{1,0:T(8,128)(2,1)S(1)}, bf16[768,1536]{1,0:T(8,128)(2,1)}, u32[]{:S(2)}) copy-start(bf16[768,1536]{1,0:T(8,128)(2,1)} %param.31) | copy-start | bytes 7077892
  176.6 46.3 %reduce-scatter.7.cloned.1.call-start = ((), (), s32[]{:S(2)}) async-start(), calls=%async_computation.7 | async-start | bytes 1806336 | tf_op jit(solution)/shard_map/reduce_scatter | solution.py:118
  186.4 36.5 %copy-start.5 = (bf16[392,768]{1,0:T(8,128)(2,1)S(1)}, bf16[392,768]{1,0:T(8,128)(2,1)}, u32[]{:S(2)}) copy-start(bf16[392,768]{1,0:T(8,128)(2,1)} %reduce-scatter.5.cloned.1.call-done) | copy-start | bytes 1806340
  186.4 36.5 %copy-start.43 = (f32[768]{0:T(1024)S(1)}, f32[768]{0:T(1024)}, u32[]{:S(2)}) copy-start(f32[768]{0:T(1024)} %param.34) | copy-start | bytes 9220
  186.5 184.3 %reduce-scatter.11.cloned.1.call-start = ((), (), s32[]{:S(2)}) async-start(), calls=%async_computation.10 | async-start | bytes 1806336 | tf_op jit(solution)/shard_map/reduce_scatter | solution.py:189
  227.0 15.5 %collective-permute-start = (bf16[1,392,768]{2,1,0:T(8,128)(2,1)S(1)}, bf16[1,392,768]{2,1,0:T(8,128)(2,1)}, u32[]{:S(2)}, u32[]{:S(2)}) collective-permute-start(bf16[1,392,768]{2,1,0:T(8,128)(2,1)S(1)} %bitcast.81), channel_id=1, source_target_pairs={{0,1},{1,0},{2,3},{3,2},{4,5},{5,4},{6,7},{7,6},{8,9},{9,8},{10,11... | collective-permute-start | bytes 1806344 | tf_op jit(solution)/shard_map/ppermute | solution.py:24
  227.4 17.4 %copy-start.49 = (bf16[384,768]{1,0:T(8,128)(2,1)S(1)}, bf16[384,768]{1,0:T(8,128)(2,1)}, u32[]{:S(2)}) copy-start(bf16[384,768]{1,0:T(8,128)(2,1)} %param.27) | copy-start | bytes 1769476
  253.3 29.0 %copy-start.13 = (bf16[6,64,784]{2,1,0:T(8,128)(2,1)}, bf16[6,64,784]{2,1,0:T(8,128)(2,1)S(1)}, u32[]{:S(2)}) copy-start(bf16[6,64,784]{2,1,0:T(8,128)(2,1)S(1)} %convolution_convert_fusion.4) | copy-start | bytes 1806340
  287.6 290.3 %all-reduce.5.cloned.1.call-start = ((), (), s32[]{:S(2)}) async-start(), calls=%async_computation.11 | async-start | bytes 28311552 | tf_op jit(solution)/shard_map/psum | solution.py:277
  305.7 65.0 %copy-start.34 = (f32[392]{0:T(512)S(1)}, f32[392]{0:T(512)}, u32[]{:S(2)}) copy-start(f32[392]{0:T(512)} %copy-done.33) | copy-start | bytes 4708
  305.7 65.0 %copy-start.35 = (f32[768]{0:T(1024)S(1)}, f32[768]{0:T(1024)}, u32[]{:S(2)}) copy-start(f32[768]{0:T(1024)} %param.20) | copy-start | bytes 9220
  305.8 66.6 %copy-start.40 = (f32[392]{0:T(512)S(1)}, f32[392]{0:T(512)}, u32[]{:S(2)}) copy-start(f32[392]{0:T(512)} %copy-done.39) | copy-start | bytes 4708
  305.8 66.6 %copy-start.38 = (f32[392]{0:T(512)S(1)}, f32[392]{0:T(512)}, u32[]{:S(2)}) copy-start(f32[392]{0:T(512)} %copy-done.37) | copy-start | bytes 4708
  (37 other events, 158.2 us)
Sparse Core Ops, SparseCore 0:
  12.4 25.7 all-gather.3
  82.6 22.0 reduce-scatter.4
  108.9 23.0 all-gather.5
  133.4 23.0 all-gather.7
  176.7 22.0 reduce-scatter.8
  200.9 22.0 reduce-scatter.6
  287.8 22.0 reduce-scatter.10
  316.1 261.7 all-reduce.4
